TPU v7x, 256 devices: a whole 4x4x8 slice. The times are simulated.
256 devices in a mesh: seq: 16 (over x, z_hi), wt: 16 (over z_lo, y, core).
Axes of the slice: x: 4, y: 4, z: 8 (z_hi: 4, z_lo: 2; z = z_hi * 2 + z_lo), core: 2. Of those that a mesh axis runs over, the one named last changes fastest.
Arguments:
- queries: bfloat16 [4096, 5120], P('seq', 'wt'), may hold values from -6 to 6
- keys: bfloat16 [4096, 5120], P('seq', 'wt'), may hold values from -6 to 6
- values: bfloat16 [4096, 5120], P('seq', 'wt'), may hold values from -6 to 6
- rates: float32 [4096], P('seq'), may hold values from 0.2 to 1.5
- w_gate: bfloat16 [5120, 5120], P('seq', 'wt'), may hold values from -0.078125 to 0.078125
- w_up: bfloat16 [5120, 5120], P('seq', 'wt'), may hold values from -0.078125 to 0.078125
- w_down: bfloat16 [5120, 5120], P('seq', 'wt'), may hold values from -0.078125 to 0.078125
Outputs:
- mixed: bfloat16 [4096, 5120], P('seq', 'wt')
- new_gate: bfloat16 [5120, 5120], P('seq', 'wt')
- new_up: bfloat16 [5120, 5120], P('seq', 'wt')
- new_down: bfloat16 [5120, 5120], P('seq', 'wt')
All inputs are finite; a program needn't handle non-finite values.
Results may differ from a plain program's by a relative error of at most 0.03.
Values may be sent and summed in bfloat16 or wider, within the bound.
No kernel may reach another device: no remote copies, remote signals or barrier semaphores. Data moves between devices by JAX's collectives and lax.ppermute only.
A program may use at most 64 MiB of HBM per device.

v0:
```python
import jax
import jax.numpy as jnp
from jax import lax
from jax.sharding import PartitionSpec as P


def contract_rows(matrix_left, matrix_right):
    return lax.dot_general(
        matrix_left, matrix_right, (((0,), (0,)), ((), ())), preferred_element_type=jnp.float32
    )


def local(queries, keys, values, rates, w_gate, w_up, w_down):
    queries_all, keys_all, values_all = (
        lax.all_gather(queries, "wt", axis=1, tiled=True),
        lax.all_gather(keys, "wt", axis=1, tiled=True),
        lax.all_gather(values, "wt", axis=1, tiled=True),
    )
    row_count = keys.shape[0]
    hidden_local = w_gate.shape[1]
    token_count = row_count * lax.axis_size("seq")
    hidden_count = hidden_local * lax.axis_size("wt")
    token_rate = rates * lax.rsqrt(jnp.float32(token_count * hidden_count))
    scaled_values = (token_rate[:, None] * values_all.astype(jnp.float32)).astype(jnp.bfloat16)
    pieces = (
        lax.all_gather(w_gate, "seq", axis=0, tiled=True),
        lax.all_gather(w_up, "seq", axis=0, tiled=True),
        lax.all_gather(w_down, "seq", axis=0, tiled=True),
    )
    key_cols = keys_all
    value_cols = scaled_values
    gate_pre = jnp.dot(key_cols, pieces[0], preferred_element_type=jnp.float32)
    up_pre = jnp.dot(key_cols, pieces[1], preferred_element_type=jnp.float32)
    hidden_grad = jnp.dot(value_cols, pieces[2], preferred_element_type=jnp.float32)
    sigmoid_gate = jax.nn.sigmoid(gate_pre)
    silu_gate = gate_pre * sigmoid_gate
    hidden_keys = (silu_gate * up_pre).astype(jnp.bfloat16)
    gate_grad = (
        hidden_grad * up_pre * sigmoid_gate * (1.0 + gate_pre * (1.0 - sigmoid_gate))
    ).astype(jnp.bfloat16)
    up_grad = (hidden_grad * silu_gate).astype(jnp.bfloat16)
    key_cols = keys_all
    value_cols = scaled_values
    grads = lax.psum_scatter(
        jnp.concatenate(
            [
                contract_rows(key_cols, gate_grad),
                contract_rows(key_cols, up_grad),
                contract_rows(value_cols, hidden_keys),
            ],
            axis=1,
        ).astype(jnp.bfloat16),
        "seq",
        scatter_dimension=0,
        tiled=True,
    ).astype(jnp.float32)
    new_gate = (w_gate.astype(jnp.float32) + grads[:, :hidden_local]).astype(jnp.bfloat16)
    new_up = (w_up.astype(jnp.float32) + grads[:, hidden_local : 2 * hidden_local]).astype(
        jnp.bfloat16
    )
    new_down = (w_down.astype(jnp.float32) + grads[:, 2 * hidden_local :]).astype(jnp.bfloat16)
    pieces = (
        lax.all_gather(new_gate, "seq", axis=0, tiled=True),
        lax.all_gather(new_up, "seq", axis=0, tiled=True),
    )
    gate_query = jnp.dot(queries_all, pieces[0], preferred_element_type=jnp.float32)
    up_query = jnp.dot(queries_all, pieces[1], preferred_element_type=jnp.float32)
    hidden_query = (jax.nn.silu(gate_query) * up_query).astype(jnp.bfloat16)
    partial_out = lax.dot_general(
        hidden_query,
        lax.all_gather(new_down, "seq", axis=0, tiled=True),
        (((1,), (1,)), ((), ())),
        preferred_element_type=jnp.float32,
    )
    mixed = lax.psum_scatter(
        partial_out.astype(jnp.bfloat16), "wt", scatter_dimension=1, tiled=True
    )
    return (mixed, new_gate, new_up, new_down)


def solution(mesh):
    return jax.shard_map(
        local,
        mesh=mesh,
        in_specs=(
            P("seq", "wt"),
            P("seq", "wt"),
            P("seq", "wt"),
            P("seq"),
            P("seq", "wt"),
            P("seq", "wt"),
            P("seq", "wt"),
        ),
        out_specs=(P("seq", "wt"), P("seq", "wt"), P("seq", "wt"), P("seq", "wt")),
        check_vma=False,
    )
```

profile of v0, /device:TPU:2, one launch (start us, length us, event | category | flops | bytes accessed | tf_op | source)
XLA Modules:
  0.0 829.8 jit_solution(17764385886914328162)
XLA Ops:
  11.3 38.7 %all-gather.14.cloned.1.call-done = bf16[256,5120]{0,1:T(8,128)(2,1)} async-done(((bf16[256,320]{0,1:T(8,128)(2,1)}), bf16[256,5120]{0,1:T(8,128)(2,1)}) %all-gather.14.cloned.1.call-update) | async-done | bytes 2621456 | tf_op jit(solution)/shard_map/all_gather | solution.py:16
  50.0 77.5 %all-gather.18.cloned.1.call-done = bf16[5120,320]{1,0:T(8,128)(2,1)} async-done(((bf16[320,320]{1,0:T(8,128)(2,1)}), bf16[5120,320]{1,0:T(8,128)(2,1)}) %all-gather.18.cloned.1.call-update) | async-done | bytes 3276816 | tf_op jit(solution)/shard_map/all_gather | solution.py:26
  127.5 4.5 fusion.23
  132.0 71.1 %all-gather.16.cloned.1.call-done = bf16[5120,320]{1,0:T(8,128)(2,1)} async-done(((bf16[320,320]{1,0:T(8,128)(2,1)}), bf16[5120,320]{1,0:T(8,128)(2,1)}) %all-gather.16.cloned.1.call-update) | async-done | bytes 3276816 | tf_op jit(solution)/shard_map/all_gather | solution.py:27
  203.1 3.7 fusion.22
  206.8 33.2 %all-gather.10.cloned.1.call-done = bf16[256,5120]{0,1:T(8,128)(2,1)} async-done(((bf16[256,320]{0,1:T(8,128)(2,1)}), bf16[256,5120]{0,1:T(8,128)(2,1)}) %all-gather.10.cloned.1.call-update) | async-done | bytes 2621456 | tf_op jit(solution)/shard_map/all_gather | solution.py:17
  240.0 77.4 %all-gather.12.cloned.1.call-done = bf16[5120,320]{1,0:T(8,128)(2,1)} async-done(((bf16[320,320]{1,0:T(8,128)(2,1)}), bf16[5120,320]{1,0:T(8,128)(2,1)}) %all-gather.12.cloned.1.call-update) | async-done | bytes 3276816 | tf_op jit(solution)/shard_map/all_gather | solution.py:28
  317.3 4.5 fusion.2
  321.8 1.1 fusion.1
  322.9 1.1 fusion
  324.6 1.1 convolution_convert_fusion
  325.7 4.5 pad_maximum_fusion
  330.3 14.3 %copy.26 = bf16[5120,960]{1,0:T(8,128)(2,1)} copy(bf16[5120,960]{0,1:T(8,128)(2,1)} %pad_maximum_fusion) | data formatting | bytes 19660800
  346.1 134.6 %reduce-scatter.7.cloned.1.call-done = bf16[320,960]{1,0:T(8,128)(2,1)} async-done(((bf16[5120,960]{1,0:T(8,128)(2,1)}), bf16[320,960]{1,0:T(8,128)(2,1)}) %reduce-scatter.7.cloned.1.call-update) | async-done | bytes 614416
  480.7 1.5 copy.27
  482.5 0.9 copy.18
  484.3 0.9 copy.22
  485.4 33.0 %all-gather.22.cloned.1.call-done = bf16[256,5120]{0,1:T(8,128)(2,1)} async-done(((bf16[256,320]{0,1:T(8,128)(2,1)}), bf16[256,5120]{0,1:T(8,128)(2,1)}) %all-gather.22.cloned.1.call-update) | async-done | bytes 2621456 | tf_op jit(solution)/shard_map/all_gather | solution.py:15
  518.4 78.1 %all-gather.20.cloned.1.call-done = bf16[5120,320]{1,0:T(8,128)(2,1)} async-done(((bf16[320,320]{1,0:T(8,128)(2,1)}), bf16[5120,320]{1,0:T(8,128)(2,1)}) %all-gather.20.cloned.1.call-update) | async-done | bytes 3276816 | tf_op jit(solution)/shard_map/all_gather | solution.py:63
  596.5 4.2 convolution_bitcast_fusion.1
  600.7 72.0 %all-gather.24.cloned.1.call-done = bf16[5120,320]{1,0:T(8,128)(2,1)} async-done(((bf16[320,320]{1,0:T(8,128)(2,1)}), bf16[5120,320]{1,0:T(8,128)(2,1)}) %all-gather.24.cloned.1.call-update) | async-done | bytes 3276816 | tf_op jit(solution)/shard_map/all_gather | solution.py:64
  672.6 76.0 %all-gather.26.cloned.1.call-done = bf16[5120,320]{1,0:T(8,128)(2,1)} async-done(((bf16[320,320]{1,0:T(8,128)(2,1)}), bf16[5120,320]{1,0:T(8,128)(2,1)}) %all-gather.26.cloned.1.call-update) | async-done | bytes 3276816 | tf_op jit(solution)/shard_map/all_gather | solution.py:71
  748.6 9.1 %convolution_convert_fusion.3 = bf16[256,5120]{0,1:T(8,128)(2,1)} fusion(bf16[5120,320]{1,0:T(8,128)(2,1)} %all-gather.26.cloned.1.call-done, bf16[5120,320]{1,0:T(8,128)(2,1)} %all-gather.24.cloned.1.call-done, bf16[256,5120]{0,1:T(8,128)(2,1)S(1)} %copy-done.4, f32[256,320]{0,1:T(8,128)S(1)} %convolution_bitcast_fusion.1), kind=kOutput, calls=%fused_computation.4 | convolution fusion | flops 1679523840 | bytes 12124160 | tf_op jit(solution)/shard_map/dot_general | solution.py:69
  757.7 65.6 %reduce-scatter.5.cloned.1.call-done = bf16[256,320]{0,1:T(8,128)(2,1)} async-done(((bf16[256,5120]{0,1:T(8,128)(2,1)}), bf16[256,320]{0,1:T(8,128)(2,1)}) %reduce-scatter.5.cloned.1.call-update) | async-done | bytes 163856 | tf_op jit(solution)/shard_map/reduce_scatter | solution.py:75
  (41 shorter events, 7.7 us)
Async XLA Ops:
  7.2 42.8 %all-gather.14.cloned.1.call-start = ((), (), s32[]{:S(2)}) async-start(), calls=%async_computation.4 | async-start | bytes 2785280 | tf_op jit(solution)/shard_map/all_gather | solution.py:16
  7.9 119.6 %all-gather.18.cloned.1.call-start = ((), (), s32[]{:S(2)}) async-start(), calls=%async_computation.6 | async-start | bytes 4177920 | tf_op jit(solution)/shard_map/all_gather | solution.py:26
  8.6 194.4 %all-gather.16.cloned.1.call-start = ((), (), s32[]{:S(2)}) async-start(), calls=%async_computation.5 | async-start | bytes 4177920 | tf_op jit(solution)/shard_map/all_gather | solution.py:27
  9.4 230.6 %all-gather.10.cloned.1.call-start = ((), (), s32[]{:S(2)}) async-start(), calls=%async_computation.2 | async-start | bytes 2785280 | tf_op jit(solution)/shard_map/all_gather | solution.py:17
  10.0 307.4 %all-gather.12.cloned.1.call-start = ((), (), s32[]{:S(2)}) async-start(), calls=%async_computation.3 | async-start | bytes 4177920 | tf_op jit(solution)/shard_map/all_gather | solution.py:28
  10.5 470.1 %reduce-scatter.7.cloned.1.call-start = ((), (), s32[]{:S(2)}) async-start(), calls=%async_computation.12 | async-start | bytes 11141120
  50.0 153.1 %copy-start = (bf16[256,5120]{0,1:T(8,128)(2,1)S(1)}, bf16[256,5120]{0,1:T(8,128)(2,1)}, u32[]{:S(2)}) copy-start(bf16[256,5120]{0,1:T(8,128)(2,1)} %all-gather.14.cloned.1.call-done) | copy-start | bytes 7864324
  322.9 1.7 copy-start.5
  344.6 0.9 copy-start.1
  344.6 1.1 copy-start.2
  344.6 1.3 copy-start.3
  344.6 173.8 %all-gather.22.cloned.1.call-start = ((), (), s32[]{:S(2)}) async-start(), calls=%async_computation.8 | async-start | bytes 2785280 | tf_op jit(solution)/shard_map/all_gather | solution.py:15
  345.3 251.1 %all-gather.20.cloned.1.call-start = ((), (), s32[]{:S(2)}) async-start(), calls=%async_computation.7 | async-start | bytes 4177920 | tf_op jit(solution)/shard_map/all_gather | solution.py:63
  483.3 189.3 %all-gather.24.cloned.1.call-start = ((), (), s32[]{:S(2)}) async-start(), calls=%async_computation.9 | async-start | bytes 4177920 | tf_op jit(solution)/shard_map/all_gather | solution.py:64
  484.3 264.4 %all-gather.26.cloned.1.call-start = ((), (), s32[]{:S(2)}) async-start(), calls=%async_computation.10 | async-start | bytes 4177920 | tf_op jit(solution)/shard_map/all_gather | solution.py:71
  485.2 338.1 %reduce-scatter.5.cloned.1.call-start = ((), (), s32[]{:S(2)}) async-start(), calls=%async_computation.11 | async-start | bytes 2785280 | tf_op jit(solution)/shard_map/reduce_scatter | solution.py:75
  518.4 230.2 %copy-start.4 = (bf16[256,5120]{0,1:T(8,128)(2,1)S(1)}, bf16[256,5120]{0,1:T(8,128)(2,1)}, u32[]{:S(2)}) copy-start(bf16[256,5120]{0,1:T(8,128)(2,1)} %all-gather.22.cloned.1.call-done) | copy-start | bytes 7864324
Sparse Core Ops, SparseCore 0:
  9.8 40.1 all-gather.13
  52.4 74.9 all-gather.17
  130.0 73.0 all-gather.15
  204.8 35.1 all-gather.9
  242.3 74.9 all-gather.11
  344.7 135.9 reduce-scatter.6
  482.5 35.8 all-gather.21
  521.5 74.9 all-gather.19
  599.6 73.0 all-gather.23
  675.5 73.0 all-gather.25
  757.8 65.4 reduce-scatter.4
where the time goes:
time: 830 us
  waiting for transfers between devices  761 us (92%)
  matrix products  29.1 us (4%)
  local copies, waits for them, and re-layouts  19.7 us (2%)
  between operations  14 us (2%)
    unnamed x12, waiting for transfers between devices  138 us
    all_gather x1, waiting for transfers between devices, local(): lax.all_gather(new_gate, 'seq', axis=0, tiled=True)  78.1 us
    all_gather x1, waiting for transfers between devices, local(): lax.all_gather(w_gate, 'seq', axis=0, tiled=True)  77.5 us
    all_gather x1, waiting for transfers between devices, local(): lax.all_gather(w_down, 'seq', axis=0, tiled=True)  77.4 us
    all_gather x1, waiting for transfers between devices, local(): lax.all_gather(new_down, 'seq', axis=0, tiled=True)  76 us
    all_gather x1, waiting for transfers between devices, local(): lax.all_gather(new_up, 'seq', axis=0, tiled=True)  72 us
    all_gather x1, waiting for transfers between devices, local(): lax.all_gather(w_up, 'seq', axis=0, tiled=True)  71.1 us
    reduce_scatter x1, waiting for transfers between devices, local(): lax.psum_scatter(partial_out.astype(jnp.bfloat16), 'wt', scatter_dimensio...  65.6 us
  transfers between devices with their start and end apart: 11, of which 11 were waited for; matrix products, arithmetic and copies ran while one was open for 2% of the time, Pallas kernels for 0%

commit v1 on v0

--- a/solution.py
+++ b/solution.py
@@ -68,7 +68,9 @@
     hidden_query = (jax.nn.silu(gate_query) * up_query).astype(jnp.bfloat16)
     partial_out = lax.dot_general(
         hidden_query,
-        lax.all_gather(new_down, "seq", axis=0, tiled=True),
+        jnp.concatenate(
+            lax.all_to_all(jnp.stack([new_down] * lax.axis_size("seq")), "seq", 0, 0), axis=0
+        ),
         (((1,), (1,)), ((), ())),
         preferred_element_type=jnp.float32,
     )

time: 830 us -> 809 us (0.975)
  waiting for transfers between devices: 761 us -> 730 us
    all_gather x1 -> x0, waiting for transfers between devices: 76 us -> none  [local(): lax.all_gather(new_down, 'seq', axis=0, tiled=True)]
    all_gather x1, waiting for transfers between devices: 33 us -> 60.4 us  [local(): lax.all_gather(queries, 'wt', axis=1, tiled=True)]
    all_gather x1, waiting for transfers between devices: 78.1 us -> 95.7 us  [local(): lax.all_gather(new_gate, 'seq', axis=0, tiled=True)]
    unnamed x12 -> x11, waiting for transfers between devices: 138 us -> 138 us
    unnamed x17 -> x19, local copies, waits for them, and re-layouts: 17.1 us -> 17.1 us
  transfers between devices with their start and end apart: 11 -> 11, of which waited for: 11 -> 10; matrix products, arithmetic and copies ran while one was open for 2% -> 2% of each run, Pallas kernels for 0% -> 0%
where the time goes in v1:
time: 809 us; the launch traced here: 808 us
  waiting for transfers between devices  730 us (90%)
  matrix products  29.1 us (4%)
  local copies, waits for them, and re-layouts  21.4 us (3%)
  between operations  14.3 us (2%)
    unnamed x11, waiting for transfers between devices  138 us
    all_gather x1, waiting for transfers between devices, local(): lax.all_gather(new_gate, 'seq', axis=0, tiled=True)  95.7 us
    all_gather x1, waiting for transfers between devices, local(): lax.all_gather(w_gate, 'seq', axis=0, tiled=True)  77.5 us
    all_gather x1, waiting for transfers between devices, local(): lax.all_gather(w_down, 'seq', axis=0, tiled=True)  77.4 us
    all_gather x1, waiting for transfers between devices, local(): lax.all_gather(new_up, 'seq', axis=0, tiled=True)  72 us
    all_gather x1, waiting for transfers between devices, local(): lax.all_gather(w_up, 'seq', axis=0, tiled=True)  71.1 us
    reduce_scatter x1, waiting for transfers between devices, local(): lax.psum_scatter(partial_out.astype(jnp.bfloat16), 'wt', scatter_dimensio...  65.6 us
    all_gather x1, waiting for transfers between devices, local(): lax.all_gather(queries, 'wt', axis=1, tiled=True)  60.4 us
  transfers between devices with their start and end apart: 11, of which 10 were waited for; matrix products, arithmetic and copies ran while one was open for 2% of the time, Pallas kernels for 0%

profile of v1, /device:TPU:2, one launch (start us, length us, event | category | flops | bytes accessed | tf_op | source)
XLA Modules:
  0.0 808.2 jit_solution(14329430505999205754)
XLA Ops:
  11.3 38.7 %all-gather.13.cloned.1.call-done = bf16[256,5120]{0,1:T(8,128)(2,1)} async-done(((bf16[256,320]{0,1:T(8,128)(2,1)}), bf16[256,5120]{0,1:T(8,128)(2,1)}) %all-gather.13.cloned.1.call-update) | async-done | bytes 2621456 | tf_op jit(solution)/shard_map/all_gather | solution.py:16
  50.0 77.5 %all-gather.17.cloned.1.call-done = bf16[5120,320]{1,0:T(8,128)(2,1)} async-done(((bf16[320,320]{1,0:T(8,128)(2,1)}), bf16[5120,320]{1,0:T(8,128)(2,1)}) %all-gather.17.cloned.1.call-update) | async-done | bytes 3276816 | tf_op jit(solution)/shard_map/all_gather | solution.py:26
  127.5 4.5 fusion.23
  132.0 71.1 %all-gather.15.cloned.1.call-done = bf16[5120,320]{1,0:T(8,128)(2,1)} async-done(((bf16[320,320]{1,0:T(8,128)(2,1)}), bf16[5120,320]{1,0:T(8,128)(2,1)}) %all-gather.15.cloned.1.call-update) | async-done | bytes 3276816 | tf_op jit(solution)/shard_map/all_gather | solution.py:27
  203.1 3.7 fusion.22
  206.8 33.2 %all-gather.9.cloned.1.call-done = bf16[256,5120]{0,1:T(8,128)(2,1)} async-done(((bf16[256,320]{0,1:T(8,128)(2,1)}), bf16[256,5120]{0,1:T(8,128)(2,1)}) %all-gather.9.cloned.1.call-update) | async-done | bytes 2621456 | tf_op jit(solution)/shard_map/all_gather | solution.py:17
  240.0 77.4 %all-gather.11.cloned.1.call-done = bf16[5120,320]{1,0:T(8,128)(2,1)} async-done(((bf16[320,320]{1,0:T(8,128)(2,1)}), bf16[5120,320]{1,0:T(8,128)(2,1)}) %all-gather.11.cloned.1.call-update) | async-done | bytes 3276816 | tf_op jit(solution)/shard_map/all_gather | solution.py:28
  317.3 4.5 fusion.2
  321.8 1.1 fusion.1
  322.9 1.1 fusion
  324.6 1.1 convolution_convert_fusion
  325.7 4.5 pad_maximum_fusion
  330.3 14.3 %copy.27 = bf16[5120,960]{1,0:T(8,128)(2,1)} copy(bf16[5120,960]{0,1:T(8,128)(2,1)} %pad_maximum_fusion) | data formatting | bytes 19660800
  346.1 134.6 %reduce-scatter.7.cloned.1.call-done = bf16[320,960]{1,0:T(8,128)(2,1)} async-done(((bf16[5120,960]{1,0:T(8,128)(2,1)}), bf16[320,960]{1,0:T(8,128)(2,1)}) %reduce-scatter.7.cloned.1.call-update) | async-done | bytes 614416
  480.7 1.5 copy.28
  483.5 2.4 stack.2
  485.9 7.3 all-to-all-start
  493.3 0.9 copy.21
  494.4 60.4 %all-gather.21.cloned.1.call-done = bf16[256,5120]{0,1:T(8,128)(2,1)} async-done(((bf16[256,320]{0,1:T(8,128)(2,1)}), bf16[256,5120]{0,1:T(8,128)(2,1)}) %all-gather.21.cloned.1.call-update) | async-done | bytes 2621456 | tf_op jit(solution)/shard_map/all_gather | solution.py:15
  554.8 95.7 %all-gather.19.cloned.1.call-done = bf16[5120,320]{1,0:T(8,128)(2,1)} async-done(((bf16[320,320]{1,0:T(8,128)(2,1)}), bf16[5120,320]{1,0:T(8,128)(2,1)}) %all-gather.19.cloned.1.call-update) | async-done | bytes 3276816 | tf_op jit(solution)/shard_map/all_gather | solution.py:63
  650.5 4.2 convolution_bitcast_fusion.1
  654.7 72.0 %all-gather.23.cloned.1.call-done = bf16[5120,320]{1,0:T(8,128)(2,1)} async-done(((bf16[320,320]{1,0:T(8,128)(2,1)}), bf16[5120,320]{1,0:T(8,128)(2,1)}) %all-gather.23.cloned.1.call-update) | async-done | bytes 3276816 | tf_op jit(solution)/shard_map/all_gather | solution.py:64
  726.6 9.1 %convolution_convert_fusion.3 = bf16[256,5120]{0,1:T(8,128)(2,1)} fusion(bf16[5120,320]{1,0:T(8,128)(2,1)} %bitcast.4, bf16[5120,320]{1,0:T(8,128)(2,1)} %all-gather.23.cloned.1.call-done, bf16[256,5120]{0,1:T(8,128)(2,1)S(1)} %copy-done.5, f32[256,320]{0,1:T(8,128)S(1)} %convolution_bitcast_fusion.1), kind=kOutput, calls=%fused_computation.4 | convolution fusion | flops 1679523840 | bytes 12124160 | tf_op jit(solution)/shard_map/dot_general | solution.py:69
  735.7 65.6 %reduce-scatter.5.cloned.1.call-done = bf16[256,320]{0,1:T(8,128)(2,1)} async-done(((bf16[256,5120]{0,1:T(8,128)(2,1)}), bf16[256,320]{0,1:T(8,128)(2,1)}) %reduce-scatter.5.cloned.1.call-update) | async-done | bytes 163856 | tf_op jit(solution)/shard_map/reduce_scatter | solution.py:77
  (43 shorter events, 7.9 us)
Async XLA Ops:
  7.2 42.8 %all-gather.13.cloned.1.call-start = ((), (), s32[]{:S(2)}) async-start(), calls=%async_computation.5 | async-start | bytes 2785280 | tf_op jit(solution)/shard_map/all_gather | solution.py:16
  7.9 119.6 %all-gather.17.cloned.1.call-start = ((), (), s32[]{:S(2)}) async-start(), calls=%async_computation.7 | async-start | bytes 4177920 | tf_op jit(solution)/shard_map/all_gather | solution.py:26
  8.6 194.4 %all-gather.15.cloned.1.call-start = ((), (), s32[]{:S(2)}) async-start(), calls=%async_computation.6 | async-start | bytes 4177920 | tf_op jit(solution)/shard_map/all_gather | solution.py:27
  9.4 230.6 %all-gather.9.cloned.1.call-start = ((), (), s32[]{:S(2)}) async-start(), calls=%async_computation.3 | async-start | bytes 2785280 | tf_op jit(solution)/shard_map/all_gather | solution.py:17
  10.0 307.4 %all-gather.11.cloned.1.call-start = ((), (), s32[]{:S(2)}) async-start(), calls=%async_computation.4 | async-start | bytes 4177920 | tf_op jit(solution)/shard_map/all_gather | solution.py:28
  10.5 470.1 %reduce-scatter.7.cloned.1.call-start = ((), (), s32[]{:S(2)}) async-start(), calls=%async_computation.12 | async-start | bytes 11141120
  50.0 153.1 %copy-start = (bf16[256,5120]{0,1:T(8,128)(2,1)S(1)}, bf16[256,5120]{0,1:T(8,128)(2,1)}, u32[]{:S(2)}) copy-start(bf16[256,5120]{0,1:T(8,128)(2,1)} %all-gather.13.cloned.1.call-done) | copy-start | bytes 7864324
  322.9 1.7 copy-start.6
  344.6 0.9 copy-start.1
  344.6 1.1 copy-start.2
  344.6 1.3 copy-start.3
  344.6 210.2 %all-gather.21.cloned.1.call-start = ((), (), s32[]{:S(2)}) async-start(), calls=%async_computation.9 | async-start | bytes 2785280 | tf_op jit(solution)/shard_map/all_gather | solution.py:15
  345.3 305.1 %all-gather.19.cloned.1.call-start = ((), (), s32[]{:S(2)}) async-start(), calls=%async_computation.8 | async-start | bytes 4177920 | tf_op jit(solution)/shard_map/all_gather | solution.py:63
  483.5 2.4 copy-start.4
  485.9 168.7 %all-to-all-start = ((bf16[16,320,320]{2,1,0:T(8,128)(2,1)}), bf16[16,320,320]{2,1,0:T(8,128)(2,1)}, u32[]{:S(2)}, u32[]{:S(2)}) async-start(bf16[16,320,320]{2,1,0:T(8,128)(2,1)} %stack.2), calls=%async_computation | async-start | bytes 7864320 | tf_op jit(solution)/shard_map/all_to_all | solution.py:72
  493.2 233.4 %all-gather.23.cloned.1.call-start = ((), (), s32[]{:S(2)}) async-start(), calls=%async_computation.10 | async-start | bytes 4177920 | tf_op jit(solution)/shard_map/all_gather | solution.py:64
  494.2 307.2 %reduce-scatter.5.cloned.1.call-start = ((), (), s32[]{:S(2)}) async-start(), calls=%async_computation.11 | async-start | bytes 2785280 | tf_op jit(solution)/shard_map/reduce_scatter | solution.py:77
  554.8 171.8 %copy-start.5 = (bf16[256,5120]{0,1:T(8,128)(2,1)S(1)}, bf16[256,5120]{0,1:T(8,128)(2,1)}, u32[]{:S(2)}) copy-start(bf16[256,5120]{0,1:T(8,128)(2,1)} %all-gather.21.cloned.1.call-done) | copy-start | bytes 7864324
Sparse Core Ops, SparseCore 0:
  9.8 40.1 all-gather.12
  52.4 74.9 all-gather.16
  130.0 73.0 all-gather.14
  204.8 35.1 all-gather.8
  242.3 74.9 all-gather.10
  344.7 135.9 reduce-scatter.6
  482.5 72.2 all-gather.20
  557.9 92.5 all-gather.18
  653.5 73.0 all-gather.22
  735.8 65.4 reduce-scatter.4
